TPU v7x, 512 devices: a whole 4x8x8 slice. The times are simulated.
512 devices in a mesh: dp: 32 (over z, y_hi), tensor: 16 (over x, y_lo, core).
Axes of the slice: x: 4, y: 8 (y_hi: 4, y_lo: 2; y = y_hi * 2 + y_lo), z: 8, core: 2. Of those that a mesh axis runs over, the one named last changes fastest.
Arguments:
- hidden: bfloat16 [16384, 7168], P('dp', 'tensor'), may hold values from -6 to 6
- w_down: bfloat16 [7168, 576], P('tensor'), may hold values from -0.0625 to 0.0625
- norm_gain: float32 [512], replicated, may hold values from 0.25 to 1.75
- w_up: bfloat16 [512, 32768], P('dp', 'tensor'), may hold values from -0.25 to 0.25
- kv_grad: bfloat16 [16384, 32768], P('dp', 'tensor'), may hold values from -6 to 6
- rope_grad: bfloat16 [16384, 64], P('dp'), may hold values from -6 to 6
Outputs:
- hidden_grad: bfloat16 [16384, 7168], P('dp', 'tensor')
- down_grad: bfloat16 [7168, 576], P('tensor')
- gain_grad: float32 [512], replicated
- up_grad: bfloat16 [512, 32768], P('dp', 'tensor')
All inputs are finite; a program needn't handle non-finite values.
Results may differ from a plain program's by a relative error of at most 0.005.
Values may be sent and summed in bfloat16 or wider, within the bound.
No kernel may reach another device: no remote copies, remote signals or barrier semaphores. Data moves between devices by JAX's collectives and lax.ppermute only.
A program may use at most 64 MiB of HBM per device.

v0:
```python
import jax
import jax.numpy as jnp
from jax import lax
from jax.sharding import PartitionSpec as P

MB = 256
MICROS = 2


def norm_back(projected, latent_grad, norm_gain, lat_width):
    inv_rms = lax.rsqrt(jnp.mean(projected * projected, axis=1, keepdims=True) + 1e-06)
    latent = (projected * inv_rms * norm_gain).astype(jnp.bfloat16)
    gain_share = jnp.sum(latent_grad * projected * inv_rms, axis=0)
    scaled = norm_gain * latent_grad
    proj_grad = (
        inv_rms * scaled
        - projected
        * inv_rms
        * inv_rms
        * inv_rms
        * jnp.sum(scaled * projected, axis=1, keepdims=True)
        / lat_width
    ).astype(jnp.bfloat16)
    return (latent, proj_grad, gain_share)


def shards(hidden, w_down, norm_gain, w_up, kv_grad, rope_grad):
    lat_width = norm_gain.shape[0]
    latent_grad_all = lax.dot_general(
        kv_grad,
        lax.all_gather(w_up, "dp", axis=0, tiled=True),
        (((1,), (1,)), ((), ())),
        preferred_element_type=jnp.float32,
    )
    up_running = jnp.zeros((lat_width, kv_grad.shape[1]), jnp.float32)
    down_running = jnp.zeros((w_down.shape[0], w_down.shape[1]), jnp.float32)
    gain_running = jnp.zeros((lat_width,), jnp.float32)
    input_grads = []
    for micro_index in range(MICROS):
        row_range = slice(micro_index * MB, (micro_index + 1) * MB)
        hidden_rows = hidden[row_range]
        cot_rows = kv_grad[row_range]
        proj_partial = jnp.dot(
            hidden_rows, w_down[:, :lat_width], preferred_element_type=jnp.float32
        )
        proj_full, lgrad_full = lax.psum((proj_partial, latent_grad_all[row_range]), "tensor")
        latent, proj_grad, gain_share = norm_back(proj_full, lgrad_full, norm_gain, lat_width)
        gain_running = gain_running + gain_share
        up_running = up_running + lax.dot_general(
            latent, cot_rows, (((0,), (0,)), ((), ())), preferred_element_type=jnp.float32
        )
        joint_grad = jnp.concatenate([proj_grad, rope_grad[row_range]], axis=1)
        down_running = down_running + lax.dot_general(
            hidden_rows, joint_grad, (((0,), (0,)), ((), ())), preferred_element_type=jnp.float32
        )
        input_grads.append(
            lax.dot_general(
                joint_grad, w_down, (((1,), (1,)), ((), ())), preferred_element_type=jnp.float32
            ).astype(jnp.bfloat16)
        )
    hidden_grad = jnp.concatenate(input_grads, axis=0)
    gain_grad = lax.psum(gain_running, "dp")
    up_grad = lax.psum_scatter(up_running, "dp", scatter_dimension=0, tiled=True).astype(
        jnp.bfloat16
    )
    down_grad = lax.psum(down_running, "dp").astype(jnp.bfloat16)
    return (hidden_grad, down_grad, gain_grad, up_grad)


def solution(mesh):
    placed = (
        P("dp", "tensor"),
        P("tensor", None),
        P(),
        P("dp", "tensor"),
        P("dp", "tensor"),
        P("dp", None),
    )
    return jax.shard_map(
        shards,
        mesh=mesh,
        in_specs=placed,
        out_specs=(P("dp", "tensor"), P("tensor", None), P(), P("dp", "tensor")),
        check_vma=False,
    )
```

profile of v0, /device:TPU:2, one launch (start us, length us, event | category | flops | bytes accessed | tf_op | source)
XLA Modules:
  0.0 486.4 jit_solution(1724037319380611540)
XLA Ops:
  7.2 0.0 all-gather.2.cloned.1.call-start
  7.2 0.7 all-gather.2.cloned.1.call-update
  7.9 0.0 all-reduce.5.cloned.1.call-start
  8.0 2.3 fusion.4
  10.2 2.3 fusion.6
  12.5 89.5 %all-gather.2.cloned.1.call-done = bf16[512,2048]{1,0:T(8,128)(2,1)} async-done(((bf16[16,2048]{1,0:T(8,128)(2,1)}), bf16[512,2048]{1,0:T(8,128)(2,1)}) %all-gather.2.cloned.1.call-update) | async-done | bytes 2097168 | tf_op jit(solution)/shard_map/all_gather | solution.py:31
  102.0 2.9 fusion.23
  104.9 1.1 fusion.21
  105.9 0.0 all-reduce.5.cloned.1.call-update
  105.9 0.0 reduce-scatter.2.cloned.1.call-start
  106.0 127.0 %all-reduce.5.cloned.1.call-done = (f32[256,512]{1,0:T(8,128)}, f32[256,512]{1,0:T(8,128)}, f32[256,512]{1,0:T(8,128)}, f32[256,512]{1,0:T(8,128)}) async-done(((f32[256,512]{1,0:T(8,128)}, f32[256,512]{1,0:T(8,128)}, f32[256,512]{1,0:T(8,128)}, f32[256,512]{1,0:T(8,128)}), (f32[256,512]{1,0:T(8,128)}, f32[256,512]{1,0:T(8,128)}, f32[256,512]{1,0:T(8,128)}, ...) | async-done | bytes 2097168 | tf_op jit(solution)/shard_map/psum | solution.py:46
  233.0 1.3 multiply_reduce_fusion.3
  234.4 1.9 fusion.2
  236.3 2.8 convolution_add_fusion
  239.1 0.0 reduce-scatter.2.cloned.1.call-update
  239.1 0.8 copy-done.8
  239.9 0.1 copy.12
  240.1 0.1 copy.13
  240.2 0.1 copy-done.2
  240.3 0.2 copy-done.3
  240.5 0.4 multiply_reduce_fusion.1
  240.9 0.4 subtract_convert_fusion.1
  241.3 0.2 copy-done.5
  241.5 0.3 fusion.12
  241.9 0.3 fusion
  242.2 0.4 copy-done.6
  242.6 0.4 convolution_convert_fusion.1
  243.0 0.4 convolution_convert_fusion
  243.3 0.8 pad_maximum_fusion
  244.1 184.4 %all-reduce.6 = (bf16[448,576]{1,0:T(8,128)(2,1)}, f32[512]{0:T(512)}) all-reduce(f32[448,576]{1,0:T(8,128)S(1)} %fusion, f32[512]{0:T(512)S(1)} %add.46), channel_id=1, replica_groups=mesh['dp'=32,'tensor'=16] {'dp'}, use_global_device_ids=true, to_apply=%region_8.0 | all-reduce | flops 258560 | bytes 1552384 | tf_op jit(solution)/shard_map/psum | solution.py:66
  428.5 49.8 %reduce-scatter.2.cloned.1.call-done = f32[16,2048]{1,0:T(8,128)} async-done(((f32[512,2048]{1,0:T(8,128)}), f32[16,2048]{1,0:T(8,128)}) %reduce-scatter.2.cloned.1.call-update) | async-done | bytes 131088 | tf_op jit(solution)/shard_map/reduce_scatter | solution.py:63
  478.3 1.5 convert_element_type.31
  (17 shorter events, 0.0 us)
Async XLA Ops:
  7.2 94.8 %copy-start.4 = (bf16[512,2048]{1,0:T(8,128)(2,1)S(1)}, bf16[512,2048]{1,0:T(8,128)(2,1)}, u32[]{:S(2)}) copy-start(bf16[512,2048]{1,0:T(8,128)(2,1)} %param.10) | copy-start | bytes 6291460
  7.2 94.8 %all-gather.2.cloned.1.call-start = ((), (), s32[]{:S(2)}) async-start(), calls=%async_computation.1 | async-start | bytes 2162688 | tf_op jit(solution)/shard_map/all_gather | solution.py:31
  7.9 225.1 %all-reduce.5.cloned.1.call-start = ((), (), s32[]{:S(2)}) async-start(), calls=%async_computation.3 | async-start | bytes 4194304 | tf_op jit(solution)/shard_map/psum | solution.py:46
  105.9 128.4 %copy-start.7 = (f32[512]{0:T(512)S(1)}, f32[512]{0:T(512)}, u32[]{:S(2)}) copy-start(f32[512]{0:T(512)} %param.8) | copy-start | bytes 6148
  105.9 372.4 %reduce-scatter.2.cloned.1.call-start = ((), (), s32[]{:S(2)}) async-start(), calls=%async_computation.2 | async-start | bytes 4325376 | tf_op jit(solution)/shard_map/reduce_scatter | solution.py:63
  234.4 1.9 copy-start.1
  239.1 0.8 copy-start.8
  239.1 1.1 copy-start
  239.1 1.2 copy-start.2
  239.1 1.4 copy-start.3
  240.5 1.0 copy-start.5
  241.5 1.1 copy-start.6
Sparse Core Ops, SparseCore 0:
  11.2 90.7 all-gather.1
  106.1 126.8 all-reduce.4
  239.3 239.0 reduce-scatter.1
where the time goes:
time: 487 us; the launch traced here: 486 us
  waiting for transfers between devices  267 us (55%)
  blocking collectives  184 us (38%)
  between operations  13.9 us (3%)
  matrix products  13.6 us (3%)
    psum x1, blocking collectives, shards(): down_grad = lax.psum(down_running, 'dp').astype(jnp.bfloat16)  184 us
    psum x1, waiting for transfers between devices, shards(): lax.psum((proj_partial, latent_grad_all[row_range]), 'tensor')  127 us
    all_gather x1, waiting for transfers between devices, shards(): lax.all_gather(w_up, 'dp', axis=0, tiled=True)  89.5 us
    reduce_scatter x1, waiting for transfers between devices, shards(): lax.psum_scatter(up_running, 'dp', scatter_dimension=0, tiled=True)  49.8 us
  transfers between devices with their start and end apart: 3, of which 3 were waited for; matrix products, arithmetic and copies ran while one was open for 2% of the time, Pallas kernels for 0%

commit v1 on v0

--- a/solution.py
+++ b/solution.py
@@ -63,7 +63,7 @@
     up_grad = lax.psum_scatter(up_running, "dp", scatter_dimension=0, tiled=True).astype(
         jnp.bfloat16
     )
-    down_grad = lax.psum(down_running, "dp").astype(jnp.bfloat16)
+    down_grad = jnp.sum(lax.all_gather(down_running, "dp"), axis=0).astype(jnp.bfloat16)
     return (hidden_grad, down_grad, gain_grad, up_grad)
 
 

time: 487 us -> 916 us (1.88)
  the two profiles are of different devices: /device:TPU:2 before, /device:TPU:10 now
where the time goes in v1:
time: 916 us
  waiting for transfers between devices  782 us (85%)
  blocking collectives  83.6 us (9%)
  other arithmetic  19.1 us (2%)
  matrix products  14.6 us (2%)
  between operations  13.9 us (2%)
    all_gather x1, waiting for transfers between devices, shards(): lax.all_gather(down_running, 'dp')  417 us
    reduce_scatter x1, waiting for transfers between devices, shards(): lax.psum_scatter(up_running, 'dp', scatter_dimension=0, tiled=True)  151 us
    psum x1, waiting for transfers between devices, shards(): lax.psum((proj_partial, latent_grad_all[row_range]), 'tensor')  124 us
    all_gather x1, waiting for transfers between devices, shards(): lax.all_gather(w_up, 'dp', axis=0, tiled=True)  89.1 us
    psum x1, blocking collectives, shards(): gain_grad = lax.psum(gain_running, 'dp')  83.6 us
  transfers between devices with their start and end apart: 4, of which 4 were waited for; matrix products, arithmetic and copies ran while one was open for 1% of the time, Pallas kernels for 0%

profile of v1, /device:TPU:10, one launch (start us, length us, event | category | flops | bytes accessed | tf_op | source)
XLA Modules:
  0.0 915.9 jit_solution(1289826922665332926)
XLA Ops:
  7.2 0.0 all-gather.4.cloned.1.call-start
  7.2 0.7 all-gather.4.cloned.1.call-update
  7.9 0.0 all-reduce.3.cloned.1.call-start
  8.0 2.3 fusion.4
  10.2 2.3 fusion.6
  12.5 89.1 %all-gather.4.cloned.1.call-done = bf16[512,2048]{1,0:T(8,128)(2,1)} async-done(((bf16[16,2048]{1,0:T(8,128)(2,1)}), bf16[512,2048]{1,0:T(8,128)(2,1)}) %all-gather.4.cloned.1.call-update) | async-done | bytes 2097168 | tf_op jit(solution)/shard_map/all_gather | solution.py:31
  101.6 2.9 fusion.23
  104.5 1.1 fusion.21
  105.6 0.0 reduce-scatter.2.cloned.1.call-start
  105.7 123.8 %all-reduce.3.cloned.1.call-done = (f32[256,512]{1,0:T(8,128)}, f32[256,512]{1,0:T(8,128)}, f32[256,512]{1,0:T(8,128)}, f32[256,512]{1,0:T(8,128)}) async-done(((f32[256,512]{1,0:T(8,128)}, f32[256,512]{1,0:T(8,128)}, f32[256,512]{1,0:T(8,128)}, f32[256,512]{1,0:T(8,128)}), (f32[256,512]{1,0:T(8,128)}, f32[256,512]{1,0:T(8,128)}, f32[256,512]{1,0:T(8,128)}, ...) | async-done | bytes 2097168 | tf_op jit(solution)/shard_map/psum | solution.py:46
  229.4 1.3 multiply_reduce_fusion.3
  230.8 1.9 fusion.2
  232.8 2.8 convolution_add_fusion
  235.7 0.0 all-gather.6.cloned.1.call-start
  235.7 0.8 copy-done.8
  236.5 0.1 copy.12
  236.6 0.1 copy.13
  236.7 0.1 copy-done.2
  236.9 0.2 copy-done.3
  237.0 0.4 multiply_reduce_fusion.1
  237.4 0.4 subtract_convert_fusion.1
  237.8 0.3 copy-done.5
  238.0 0.3 fusion.12
  238.4 1.4 fusion
  239.8 83.6 %psum.39 = f32[512]{0:T(512)} all-reduce(f32[512]{0:T(512)S(1)} %add.44), channel_id=1, replica_groups=mesh['dp'=32,'tensor'=16] {'dp'}, use_global_device_ids=true, to_apply=%region_11.0 | all-reduce | flops 512 | bytes 4096 | tf_op jit(solution)/shard_map/psum | solution.py:62
  323.4 0.4 convolution_convert_fusion.1
  323.8 0.4 convolution_convert_fusion
  324.2 0.8 pad_maximum_fusion
  325.0 150.7 %reduce-scatter.2.cloned.1.call-done = f32[16,2048]{1,0:T(8,128)} async-done(((f32[512,2048]{1,0:T(8,128)}), f32[16,2048]{1,0:T(8,128)}) %reduce-scatter.2.cloned.1.call-update) | async-done | bytes 131088 | tf_op jit(solution)/shard_map/reduce_scatter | solution.py:63
  475.7 1.5 convert_element_type.31
  477.2 417.5 %all-gather.6.cloned.1.call-done = f32[14336,576]{1,0:T(8,128)} async-done(((f32[448,576]{1,0:T(8,128)}), f32[14336,576]{1,0:T(8,128)}) %all-gather.6.cloned.1.call-update) | async-done | bytes 33030160 | tf_op jit(solution)/shard_map/all_gather | solution.py:66
  894.7 14.7 %reduce_sum.67 = bf16[448,576]{1,0:T(8,128)(2,1)} reduce(f32[32,448,576]{2,1,0:T(8,128)} %bitcast.7, f32[]{:T(128)} %constant.8.clone.1), dimensions={0}, to_apply=%region_8.0 | reduce | flops 7999488 | bytes 33546244 | tf_op jit(solution)/shard_map/reduce_sum | solution.py:66
  (21 shorter events, 0.1 us)
Async XLA Ops:
  7.2 94.5 %copy-start.4 = (bf16[512,2048]{1,0:T(8,128)(2,1)S(1)}, bf16[512,2048]{1,0:T(8,128)(2,1)}, u32[]{:S(2)}) copy-start(bf16[512,2048]{1,0:T(8,128)(2,1)} %param.10) | copy-start | bytes 6291460
  7.2 94.5 %all-gather.4.cloned.1.call-start = ((), (), s32[]{:S(2)}) async-start(), calls=%async_computation.1 | async-start | bytes 2162688 | tf_op jit(solution)/shard_map/all_gather | solution.py:31
  7.9 221.5 %all-reduce.3.cloned.1.call-start = ((), (), s32[]{:S(2)}) async-start(), calls=%async_computation.4 | async-start | bytes 4194304 | tf_op jit(solution)/shard_map/psum | solution.py:46
  105.6 125.2 %copy-start.7 = (f32[512]{0:T(512)S(1)}, f32[512]{0:T(512)}, u32[]{:S(2)}) copy-start(f32[512]{0:T(512)} %param.8) | copy-start | bytes 6148
  105.6 370.1 %reduce-scatter.2.cloned.1.call-start = ((), (), s32[]{:S(2)}) async-start(), calls=%async_computation.2 | async-start | bytes 4325376 | tf_op jit(solution)/shard_map/reduce_scatter | solution.py:63
  230.8 1.9 copy-start.1
  235.6 0.8 copy-start.8
  235.6 1.1 copy-start
  235.6 1.2 copy-start.2
  235.6 1.4 copy-start.3
  235.7 659.0 %all-gather.6.cloned.1.call-start = ((), (), s32[]{:S(2)}) async-start(), calls=%async_computation.3 | async-start | bytes 37847040 | tf_op jit(solution)/shard_map/all_gather | solution.py:66
  237.0 1.0 copy-start.5
  238.4 85.1 %copy-start.6 = (bf16[448,576]{1,0:T(8,128)(2,1)S(1)}, bf16[448,576]{1,0:T(8,128)(2,1)}, u32[]{:S(2)}) copy-start(bf16[448,576]{1,0:T(8,128)(2,1)} %param.7) | copy-start | bytes 1548292
Sparse Core Ops, SparseCore 0:
  11.2 90.4 all-gather.3
  105.7 123.6 all-reduce.2
  235.8 239.8 reduce-scatter.1
  479.2 415.4 all-gather.5
